TPU v7x, 512 devices: a whole 4x4x16 slice. The times are simulated.
512 devices in a mesh: tm: 8 (over y, core), space: 64 (over z, x).
Axes of the slice: x: 4, y: 4, z: 16, core: 2. Of those that a mesh axis runs over, the one named last changes fastest.
Arguments:
- snapshots: bfloat16 [128, 128, 16384], P('tm', None, 'space'), as said below
- frequencies: int32 [16], replicated, may hold values from 1 to 63, as said below
- offsets: int32 [128], P('tm'), may hold values from 0 to 16383
Outputs:
- modes: float32 [16, 2, 128, 16384], P('tm', None, None, 'space')
Inputs may be any that keep to these rules, and one draw needn't show every extreme that they name: `frequencies`: the kept frequency indices are distinct and include 1 and 63. `snapshots`: snapshot values of the record.
All inputs are finite; a program needn't handle non-finite values.
Results may differ from a plain program's by a relative error of at most 0.0041.
Values may be sent and summed in bfloat16 or wider, within the bound.
A program may use at most 64 MiB of HBM per device.

v0:
```python
import math
import jax
import jax.numpy as jnp
from jax import lax
from jax.sharding import PartitionSpec as P


def make_angle_table(frequencies, length):
    positions = jnp.arange(length, dtype=jnp.int32)
    turn_counts = frequencies[None, :] * positions[:, None] % length
    radians = turn_counts.astype(jnp.float32) * (2.0 * math.pi / length)
    window = 0.5 - 0.5 * jnp.cos(positions.astype(jnp.float32) * (2.0 * math.pi / length))
    cosine_cols = window[:, None] * jnp.cos(radians)
    sine_cols = window[:, None] * jnp.sin(radians)
    return jnp.concatenate([cosine_cols, sine_cols], axis=1).astype(jnp.bfloat16)


def embed_gram(gram_real, gram_imag):
    top_rows = jnp.stack([gram_real, -gram_imag], axis=-1)
    low_rows = jnp.stack([gram_imag, gram_real], axis=-1)
    order = gram_real.shape[0]
    return jnp.stack([top_rows, low_rows], axis=1).reshape(2 * order, 2 * order)


def local_gram(real_rows, imag_rows):
    real_gram = jnp.dot(real_rows, real_rows.T, preferred_element_type=jnp.float32) + jnp.dot(
        imag_rows, imag_rows.T, preferred_element_type=jnp.float32
    )
    cross = jnp.dot(imag_rows, real_rows.T, preferred_element_type=jnp.float32)
    imag_gram = cross - cross.T
    return jnp.stack([real_gram, imag_gram])


def unpack_gram(packed):
    return (packed[0], packed[1])


def finish_modes(packed, real_rows, imag_rows, total_cells):
    gram_real, gram_imag = unpack_gram(packed)
    embedded = embed_gram(gram_real / total_cells, gram_imag / total_cells)
    lower_factor = jnp.linalg.cholesky(embedded)
    order = real_rows.shape[0]
    cells_here = real_rows.shape[1]
    stacked_rows = (
        jnp.stack([real_rows, imag_rows], axis=1).reshape(2 * order, cells_here).astype(jnp.float32)
    )
    solved = lax.linalg.triangular_solve(lower_factor, stacked_rows, left_side=True, lower=True)
    return jnp.transpose(solved.reshape(order, 2, cells_here), (1, 0, 2))


def local(snapshots, frequencies, offsets):
    length = snapshots.shape[1]
    count_all = frequencies.shape[0]
    angle_table = make_angle_table(frequencies, length)
    projected = jnp.einsum(
        "btc,tk->kbc", snapshots, angle_table, preferred_element_type=jnp.float32
    )
    cos_part = projected[:count_all]
    sin_part = projected[count_all:]
    turn_counts = frequencies[:, None] * offsets[None, :] % length
    phase = turn_counts.astype(jnp.float32) * (2.0 * math.pi / length)
    cos_phase = jnp.cos(phase)[:, :, None]
    sin_phase = jnp.sin(phase)[:, :, None]
    real_part = cos_part * cos_phase - sin_part * sin_phase
    imag_part = -(sin_part * cos_phase + cos_part * sin_phase)
    stacked = jnp.stack([real_part, imag_part]).astype(jnp.bfloat16)
    regrouped = lax.all_to_all(stacked, "tm", split_axis=1, concat_axis=2, tiled=True)
    cells_here = regrouped.shape[3]
    total_cells = cells_here * lax.axis_size("space")
    per_freq = [
        (regrouped[0, slot_index], regrouped[1, slot_index])
        for slot_index in range(regrouped.shape[1])
    ]
    local_grams = jnp.stack([local_gram(real_rows, imag_rows) for real_rows, imag_rows in per_freq])
    summed = lax.psum(local_grams, "space")
    results = [
        finish_modes(
            summed[slot_index], per_freq[slot_index][0], per_freq[slot_index][1], total_cells
        )
        for slot_index in range(len(per_freq))
    ]
    return jnp.stack(results)


def solution(mesh):
    placed = (P("tm", None, "space"), P(), P("tm"))
    return jax.shard_map(
        local, mesh=mesh, in_specs=placed, out_specs=P("tm", None, None, "space"), check_vma=False
    )
```

profile of v0, /device:TPU:8, one launch (start us, length us, event | category | flops | bytes accessed | tf_op | source)
XLA Modules:
  0.0 465.1 jit_solution(17110627762532385624)
XLA Ops:
  6.6 0.9 multiply_convert_fusion.1
  9.5 9.1 %all-to-all-start = ((bf16[2,16,16,256]{3,2,0,1:T(8,128)(2,1)}), bf16[2,16,16,256]{3,2,0,1:T(8,128)(2,1)S(1)}, u32[]{:S(2)}, u32[]{:S(2)}) async-start(bf16[2,16,16,256]{3,2,0,1:T(8,128)(2,1)} %copy.34), calls=%async_computation | async-start | bytes 524288 | tf_op jit(solution)/shard_map/all_to_all | solution.py:67
  18.7 6.1 %all-to-all-done = bf16[2,16,16,256]{3,2,0,1:T(8,128)(2,1)S(1)} async-done(((bf16[2,16,16,256]{3,2,0,1:T(8,128)(2,1)}), bf16[2,16,16,256]{3,2,0,1:T(8,128)(2,1)S(1)}, u32[]{:S(2)}, u32[]{:S(2)}) %all-to-all-start) | async-done | bytes 262176 | tf_op jit(solution)/shard_map/all_to_all | solution.py:67
  27.7 261.0 %all-reduce.3.cloned.1.call-done = f32[2,2,128,128]{3,2,1,0:T(8,128)} async-done(((f32[2,2,128,128]{3,2,1,0:T(8,128)}), f32[2,2,128,128]{3,2,1,0:T(8,128)}) %all-reduce.3.cloned.1.call-update) | async-done | bytes 262160 | tf_op jit(solution)/shard_map/psum | solution.py:75
  288.7 1.0 fusion.20
  289.6 0.9 fusion.61
  290.6 8.8 %copy.39 = f32[128,2,128,2]{3,2,1,0:T(8,128)} copy(f32[128,2,128,2]{2,0,3,1:T(8,128)S(1)} %pad_maximum_fusion.3) | data formatting | bytes 524288 | tf_op jit(solution)/shard_map/stack | solution.py:22
  299.4 12.7 %reshape.178 = f32[256,256]{1,0:T(8,128)S(1)} reshape(f32[128,2,128,2]{3,2,1,0:T(8,128)} %copy.39) | data formatting | bytes 524288 | tf_op jit(solution)/shard_map/reshape | solution.py:22
  312.3 11.7 %cholesky.130 = f32[128,128]{1,0:T(8,128)S(1)} custom-call(f32[128,128]{1,0:T(8,128)S(1)} %cholesky.194), custom_call_target="Cholesky" | custom-call | tf_op jit(solution)/shard_map/jit(cholesky)/cholesky | solution.py:41
  324.1 9.8 %custom-call.13 = f32[1,128,128]{1,2,0:T(8,128)S(1)} custom-call(f32[1,128,128]{2,1,0:T(8,128)S(1)} %get-tuple-element.58), custom_call_target="InvertDiagBlocksLowerTriangular" | custom-call | tf_op jit(solution)/shard_map/jit(cholesky)/cholesky | solution.py:41
  334.4 11.7 %cholesky.147 = f32[128,128]{1,0:T(8,128)S(1)} custom-call(f32[128,128]{1,0:T(8,128)S(1)} %convolution_subtract_fusion.3), custom_call_target="Cholesky" | custom-call | tf_op jit(solution)/shard_map/jit(cholesky)/cholesky | solution.py:41
  348.9 4.1 while.4
  349.6 1.4 bitcast_dynamic-update-slice_fusion.4
  351.6 1.4 bitcast_dynamic-update-slice_fusion.4
  353.0 19.9 %custom-call.14 = f32[2,128,128]{1,2,0:T(8,128)S(1)} custom-call(f32[2,128,128]{2,1,0:T(8,128)S(1)} %get-tuple-element.21), custom_call_target="InvertDiagBlocksLowerTriangular" | custom-call | tf_op jit(solution)/shard_map/triangular_solve/custom-call.0 | solution.py:47
  374.1 8.7 %copy.43 = f32[128,2,128,2]{3,2,1,0:T(8,128)} copy(f32[128,2,128,2]{2,0,3,1:T(8,128)S(1)} %pad_maximum_fusion.5) | data formatting | bytes 524288 | tf_op jit(solution)/shard_map/stack | solution.py:22
  382.8 12.7 %reshape.180 = f32[256,256]{1,0:T(8,128)S(1)} reshape(f32[128,2,128,2]{3,2,1,0:T(8,128)} %copy.43) | data formatting | bytes 524288 | tf_op jit(solution)/shard_map/reshape | solution.py:22
  395.7 11.7 %cholesky.164 = f32[128,128]{1,0:T(8,128)S(1)} custom-call(f32[128,128]{1,0:T(8,128)S(1)} %cholesky.197), custom_call_target="Cholesky" | custom-call | tf_op jit(solution)/shard_map/jit(cholesky)/cholesky | solution.py:41
  407.4 9.8 %custom-call.15 = f32[1,128,128]{1,2,0:T(8,128)S(1)} custom-call(f32[1,128,128]{2,1,0:T(8,128)S(1)} %get-tuple-element.64), custom_call_target="InvertDiagBlocksLowerTriangular" | custom-call | tf_op jit(solution)/shard_map/jit(cholesky)/cholesky | solution.py:41
  417.7 11.7 %cholesky.181 = f32[128,128]{1,0:T(8,128)S(1)} custom-call(f32[128,128]{1,0:T(8,128)S(1)} %convolution_subtract_fusion.2), custom_call_target="Cholesky" | custom-call | tf_op jit(solution)/shard_map/jit(cholesky)/cholesky | solution.py:41
  432.2 4.1 while.5
  432.9 1.4 bitcast_dynamic-update-slice_fusion.5
  434.9 1.4 bitcast_dynamic-update-slice_fusion.5
  436.4 19.9 %custom-call.16 = f32[2,128,128]{1,2,0:T(8,128)S(1)} custom-call(f32[2,128,128]{2,1,0:T(8,128)S(1)} %get-tuple-element.22), custom_call_target="InvertDiagBlocksLowerTriangular" | custom-call | tf_op jit(solution)/shard_map/triangular_solve/custom-call.0 | solution.py:47
  (80 shorter events, 14.6 us)
Async XLA Ops:
  6.5 1.7 copy-start
  9.5 15.3 %all-to-all-start = ((bf16[2,16,16,256]{3,2,0,1:T(8,128)(2,1)}), bf16[2,16,16,256]{3,2,0,1:T(8,128)(2,1)S(1)}, u32[]{:S(2)}, u32[]{:S(2)}) async-start(bf16[2,16,16,256]{3,2,0,1:T(8,128)(2,1)} %copy.34), calls=%async_computation | async-start | bytes 524288 | tf_op jit(solution)/shard_map/all_to_all | solution.py:67
  18.6 270.0 %all-reduce.3.cloned.1.call-start = ((), (), s32[]{:S(2)}) async-start(), calls=%async_computation.1 | async-start | bytes 524288 | tf_op jit(solution)/shard_map/psum | solution.py:75
Sparse Core Ops, SparseCore 0:
  26.9 261.7 all-reduce.2
where the time goes:
time: 466 us; the launch traced here: 465 us
  waiting for transfers between devices  267 us (57%)
  other arithmetic  115 us (25%)
  local copies, waits for them, and re-layouts  53.6 us (12%)
  between operations  16.5 us (4%)
  starting transfers between devices  9.15 us (2%)
    psum x1, waiting for transfers between devices, local(): summed = lax.psum(local_grams, 'space')  261 us
    another operation x14, other arithmetic, finish_modes(): lower_factor = jnp.linalg.cholesky(embedded)  69.3 us
    another operation x7, other arithmetic, finish_modes(): lax.linalg.triangular_solve(lower_factor, stacked_rows, left_side=True, l...  39.9 us
    reshape x4, local copies, waits for them, and re-layouts, embed_gram(): return jnp.stack([top_rows, low_rows], axis=1).reshape(2 * order, 2 * order)  25.6 us
    another operation x2, local copies, waits for them, and re-layouts, embed_gram(): return jnp.stack([top_rows, low_rows], axis=1).reshape(2 * order, 2 * order)  17.5 us
  transfers between devices with their start and end apart: 2, of which 2 were waited for; matrix products, arithmetic and copies ran while one was open for 0% of the time, Pallas kernels for 0%

commit v1 on v0

--- a/solution.py
+++ b/solution.py
@@ -72,7 +72,7 @@
         for slot_index in range(regrouped.shape[1])
     ]
     local_grams = jnp.stack([local_gram(real_rows, imag_rows) for real_rows, imag_rows in per_freq])
-    summed = lax.psum(local_grams, "space")
+    summed = jnp.sum(lax.all_gather(local_grams, "space"), axis=0)
     results = [
         finish_modes(
             summed[slot_index], per_freq[slot_index][0], per_freq[slot_index][1], total_cells

time: 466 us -> 401 us (0.86)
  the two profiles are of different devices: /device:TPU:8 before, /device:TPU:1 now
where the time goes in v1:
time: 401 us
  waiting for transfers between devices  192 us (48%)
  other arithmetic  120 us (30%)
  local copies, waits for them, and re-layouts  52.8 us (13%)
  between operations  16.5 us (4%)
  blocking collectives  15.8 us (4%)
    all_gather x1, waiting for transfers between devices, local(): summed = jnp.sum(lax.all_gather(local_grams, 'space'), axis=0)  192 us
    another operation x14, other arithmetic, finish_modes(): lower_factor = jnp.linalg.cholesky(embedded)  69.3 us
    another operation x7, other arithmetic, finish_modes(): lax.linalg.triangular_solve(lower_factor, stacked_rows, left_side=True, l...  39.9 us
    reshape x4, local copies, waits for them, and re-layouts, embed_gram(): return jnp.stack([top_rows, low_rows], axis=1).reshape(2 * order, 2 * order)  25.8 us
    another operation x2, local copies, waits for them, and re-layouts, embed_gram(): return jnp.stack([top_rows, low_rows], axis=1).reshape(2 * order, 2 * order)  17.3 us
    all_to_all x1, blocking collectives, local(): lax.all_to_all(stacked, 'tm', split_axis=1, concat_axis=2, tiled=True)  15.8 us
    another operation x15, local copies, waits for them, and re-layouts, finish_modes(): lax.linalg.triangular_solve(lower_factor, stacked_rows, left_side=True, l...  8.21 us
  transfers between devices with their start and end apart: 1, of which 1 were waited for; matrix products, arithmetic and copies ran while one was open for 0% of the time, Pallas kernels for 0%

profile of v1, /device:TPU:1, one launch (start us, length us, event | category | flops | bytes accessed | tf_op | source)
XLA Modules:
  0.0 400.5 jit_solution(8221297225425109200)
XLA Ops:
  6.6 0.9 multiply_convert_fusion.1
  7.5 0.8 fusion.59
  8.8 15.8 %all_to_all.18 = bf16[2,16,16,256]{3,2,0,1:T(8,128)(2,1)S(1)} all-to-all(bf16[2,16,16,256]{3,2,0,1:T(8,128)(2,1)S(1)} %copy.34), channel_id=1, replica_groups=mesh['tm'=8,'space'=64] {'tm'}, dimensions={1} | all-to-all | bytes 524288 | tf_op jit(solution)/shard_map/all_to_all | solution.py:67
  27.5 191.8 %all-gather.3.cloned.1.call-done = f32[128,2,128,128]{3,2,1,0:T(8,128)} async-done(((f32[2,2,128,128]{3,2,1,0:T(8,128)}), f32[128,2,128,128]{3,2,1,0:T(8,128)}) %all-gather.3.cloned.1.call-update) | async-done | bytes 16777232 | tf_op jit(solution)/shard_map/all_gather | solution.py:75
  219.3 6.6 %reduce_sum.9 = f32[2,2,128,128]{3,2,1,0:T(8,128)S(1)} reduce(f32[64,2,2,128,128]{4,3,2,1,0:T(8,128)} %bitcast.157, f32[]{:T(128)} %constant.90.clone.1), dimensions={0}, to_apply=%region_0.1 | reduce | flops 4128768 | bytes 17039364 | tf_op jit(solution)/shard_map/reduce_sum | solution.py:75
  226.0 8.7 %copy.39 = f32[128,2,128,2]{3,2,1,0:T(8,128)} copy(f32[128,2,128,2]{2,0,3,1:T(8,128)S(1)} %pad_maximum_fusion.3) | data formatting | bytes 524288 | tf_op jit(solution)/shard_map/stack | solution.py:22
  234.7 12.9 %reshape.178 = f32[256,256]{1,0:T(8,128)S(1)} reshape(f32[128,2,128,2]{3,2,1,0:T(8,128)} %copy.39) | data formatting | bytes 524288 | tf_op jit(solution)/shard_map/reshape | solution.py:22
  247.7 11.7 %cholesky.130 = f32[128,128]{1,0:T(8,128)S(1)} custom-call(f32[128,128]{1,0:T(8,128)S(1)} %cholesky.194), custom_call_target="Cholesky" | custom-call | tf_op jit(solution)/shard_map/jit(cholesky)/cholesky | solution.py:41
  259.5 9.8 %custom-call.13 = f32[1,128,128]{1,2,0:T(8,128)S(1)} custom-call(f32[1,128,128]{2,1,0:T(8,128)S(1)} %get-tuple-element.58), custom_call_target="InvertDiagBlocksLowerTriangular" | custom-call | tf_op jit(solution)/shard_map/jit(cholesky)/cholesky | solution.py:41
  269.8 11.7 %cholesky.147 = f32[128,128]{1,0:T(8,128)S(1)} custom-call(f32[128,128]{1,0:T(8,128)S(1)} %convolution_subtract_fusion.3), custom_call_target="Cholesky" | custom-call | tf_op jit(solution)/shard_map/jit(cholesky)/cholesky | solution.py:41
  284.4 4.1 %while.4 = (s32[]{:T(128)}, f32[256,256]{1,0:T(8,128)S(1)}, s32[2,2]{1,0:T(2,128)S(1)}, f32[2,128,128]{2,1,0:T(8,128)S(1)}, s32[]{:T(128)}) while((s32[]{:T(128)}, f32[256,256]{1,0:T(8,128)S(1)}, s32[2,2]{1,0:T(2,128)S(1)}, f32[2,128,128]{2,1,0:T(8,128)S(1)}, s32[]{:T(128)}) %tuple.59), condition=%wide.while_cond, body=%wide.while_body.sunk | while | flops 2 | bytes 131181 | solution.py:47
  285.0 1.4 bitcast_dynamic-update-slice_fusion.4
  287.1 1.4 bitcast_dynamic-update-slice_fusion.4
  288.5 19.9 %custom-call.14 = f32[2,128,128]{1,2,0:T(8,128)S(1)} custom-call(f32[2,128,128]{2,1,0:T(8,128)S(1)} %get-tuple-element.21), custom_call_target="InvertDiagBlocksLowerTriangular" | custom-call | tf_op jit(solution)/shard_map/triangular_solve/custom-call.0 | solution.py:47
  309.6 8.7 %copy.43 = f32[128,2,128,2]{3,2,1,0:T(8,128)} copy(f32[128,2,128,2]{2,0,3,1:T(8,128)S(1)} %pad_maximum_fusion.5) | data formatting | bytes 524288 | tf_op jit(solution)/shard_map/stack | solution.py:22
  318.2 12.7 %reshape.180 = f32[256,256]{1,0:T(8,128)S(1)} reshape(f32[128,2,128,2]{3,2,1,0:T(8,128)} %copy.43) | data formatting | bytes 524288 | tf_op jit(solution)/shard_map/reshape | solution.py:22
  331.1 11.7 %cholesky.164 = f32[128,128]{1,0:T(8,128)S(1)} custom-call(f32[128,128]{1,0:T(8,128)S(1)} %cholesky.197), custom_call_target="Cholesky" | custom-call | tf_op jit(solution)/shard_map/jit(cholesky)/cholesky | solution.py:41
  342.9 9.8 %custom-call.15 = f32[1,128,128]{1,2,0:T(8,128)S(1)} custom-call(f32[1,128,128]{2,1,0:T(8,128)S(1)} %get-tuple-element.64), custom_call_target="InvertDiagBlocksLowerTriangular" | custom-call | tf_op jit(solution)/shard_map/jit(cholesky)/cholesky | solution.py:41
  353.2 11.7 %cholesky.181 = f32[128,128]{1,0:T(8,128)S(1)} custom-call(f32[128,128]{1,0:T(8,128)S(1)} %convolution_subtract_fusion.2), custom_call_target="Cholesky" | custom-call | tf_op jit(solution)/shard_map/jit(cholesky)/cholesky | solution.py:41
  367.7 4.1 %while.5 = (s32[]{:T(128)}, f32[256,256]{1,0:T(8,128)S(1)}, s32[2,2]{1,0:T(2,128)S(1)}, f32[2,128,128]{2,1,0:T(8,128)S(1)}, s32[]{:T(128)}) while((s32[]{:T(128)}, f32[256,256]{1,0:T(8,128)S(1)}, s32[2,2]{1,0:T(2,128)S(1)}, f32[2,128,128]{2,1,0:T(8,128)S(1)}, s32[]{:T(128)}) %tuple.64), condition=%wide.while_cond.clone, body=%wide.while_body.clone.sunk | while | flops 2 | bytes 131181 | solution.py:47
  368.3 1.4 bitcast_dynamic-update-slice_fusion.5
  370.4 1.4 bitcast_dynamic-update-slice_fusion.5
  371.8 19.9 %custom-call.16 = f32[2,128,128]{1,2,0:T(8,128)S(1)} custom-call(f32[2,128,128]{2,1,0:T(8,128)S(1)} %get-tuple-element.22), custom_call_target="InvertDiagBlocksLowerTriangular" | custom-call | tf_op jit(solution)/shard_map/triangular_solve/custom-call.0 | solution.py:47
  392.9 0.8 pad_maximum_fusion
  (80 shorter events, 12.3 us)
Async XLA Ops:
  6.5 1.7 copy-start
  6.5 212.7 %all-gather.3.cloned.1.call-start = ((), (), s32[]{:S(2)}) async-start(), calls=%async_computation.1 | async-start | bytes 17039360 | tf_op jit(solution)/shard_map/all_gather | solution.py:75
Sparse Core Ops, SparseCore 0:
  26.7 192.4 all-gather.2
